TPU v7x, 32 devices: a whole 2x2x4 slice. The times are simulated.
32 devices in a mesh: shard: 4 (over z), ctx: 4 (over y, x), tp: 2 (over core).
Axes of the slice: x: 2, y: 2, z: 4, core: 2. Of those that a mesh axis runs over, the one named last changes fastest.
Arguments:
- tokens: bfloat16 [4, 4096, 1024], P('shard', 'ctx'), may hold values from -6 to 6
- lengths: int32 [4], P('shard'), may hold values from 1024 to 4096, as said below
- routes: int32 [4, 4096, 1], P('shard', 'ctx'), may hold values from 0 to 15
- query_key_value_weight: bfloat16 [3, 1024, 1024], P(None, ('shard', 'ctx'), 'tp'), may hold values from -0.1875 to 0.1875
- context_blend_linear_map: bfloat16 [1024, 1024], P(('shard', 'ctx'), 'tp'), may hold values from -3 to 3
- router: bfloat16 [1024, 16], P(('shard', 'ctx')), may hold values from -0.09375 to 0.09375
- gain_one: bfloat16 [1024], P(('shard', 'ctx')), may hold values from 0.5 to 1.5
- gain_two: bfloat16 [1024], P(('shard', 'ctx')), may hold values from 0.5 to 1.5
- w_in: bfloat16 [16, 1024, 4096], P(('shard', 'ctx'), None, 'tp'), may hold values from -0.1875 to 0.1875
- w_out: bfloat16 [16, 4096, 1024], P(('shard', 'ctx'), 'tp'), may hold values from -1.5 to 1.5
- cotangent: bfloat16 [4, 4096, 1024], P('shard', 'ctx'), may hold values from -6 to 6
Outputs:
- output: bfloat16 [4, 4096, 1024], P('shard', 'ctx')
- grad_tokens: float32 [4, 4096, 1024], P('shard', 'ctx')
- grad_w_qkv: float32 [3, 1024, 1024], P(None, ('shard', 'ctx'), 'tp')
- grad_attn_proj: float32 [1024, 1024], P(('shard', 'ctx'), 'tp')
- grad_router: float32 [1024, 16], P(('shard', 'ctx'))
- grad_gain_one: float32 [1024], P(('shard', 'ctx'))
- grad_gain_two: float32 [1024], P(('shard', 'ctx'))
- grad_w_in: float32 [16, 1024, 4096], P(('shard', 'ctx'), None, 'tp')
- grad_w_out: float32 [16, 4096, 1024], P(('shard', 'ctx'), 'tp')
Inputs may be any that keep to these rules, and one draw needn't show every extreme that they name: `lengths`: at least one slot has all 4096 positions used.
All inputs are finite; a program needn't handle non-finite values.
Results may differ from a plain program's by a relative error of at most 0.03.
Values may be sent and summed in bfloat16 or wider, within the bound.
A program may use at most 256 MiB of HBM per device.

v0:
```python
import math
import jax
import jax.numpy as jnp
from jax import lax
from jax.sharding import PartitionSpec as P

HEAD_DIM = 64
epsilon = 1e-05
masked_score = -1e30
key_block = 512


def norm_parts(values, gain):
    center = values - jnp.mean(values, axis=-1, keepdims=True)
    multiplier_coefficient = lax.rsqrt(jnp.mean(center * center, axis=-1, keepdims=True) + epsilon)
    normed = center * multiplier_coefficient
    return (normed * gain, normed, multiplier_coefficient)


def norm_back(grad, normed, multiplier_coefficient, gain):
    scaled = grad * gain
    inner = (
        scaled
        - jnp.mean(scaled, axis=-1, keepdims=True)
        - normed * jnp.mean(scaled * normed, axis=-1, keepdims=True)
    )
    return (inner * multiplier_coefficient, jnp.sum(grad * normed, axis=0))


def score_block(query, block, begin, query_places, lengths, heads):
    slots, block_len, twice = block.shape
    half = twice // 2
    keys = block[:, :, :half].reshape(slots, block_len, heads, HEAD_DIM)
    values = block[:, :, half:].reshape(slots, block_len, heads, HEAD_DIM)
    key_places = begin + jnp.arange(block_len, dtype=jnp.int32)
    allowed = (key_places[None, None, :] <= query_places[None, :, None]) & (
        key_places[None, None, :] < lengths[:, None, None]
    )
    scores = jnp.einsum(
        "sqhd,skhd->sqhk", query, keys, preferred_element_type=jnp.float32
    ) * HEAD_DIM ** (-0.5)
    return (keys, values, allowed[:, :, None, :], scores)


def contract_rows(left, right):
    return lax.dot_general(
        left, right, (((0,), (0,)), ((), ())), preferred_element_type=jnp.float32
    )


def contract_cols(left, right):
    return lax.dot_general(
        left, right, (((1,), (1,)), ((), ())), preferred_element_type=jnp.float32
    )


def local(
    tokens,
    lengths,
    routes,
    query_key_value_weight,
    context_blend_linear_map,
    router,
    gain_one,
    gain_two,
    w_in,
    w_out,
    cotangent,
):
    slots, local_len, width = tokens.shape
    count = slots * local_len
    head_width = query_key_value_weight.shape[2]
    heads = head_width // HEAD_DIM
    experts = router.shape[1]
    capacity = max(2, (5 * count + 4 * experts - 1) // (4 * experts))
    scale = HEAD_DIM ** (-0.5)
    ctx_rank = lax.axis_index("ctx")
    query_places = ctx_rank * local_len + jnp.arange(local_len, dtype=jnp.int32)
    full_qkv, full_proj, full_router, full_one, full_two = (
        lax.all_gather(query_key_value_weight, ("shard", "ctx"), axis=1, tiled=True),
        lax.all_gather(context_blend_linear_map, ("shard", "ctx"), axis=0, tiled=True),
        lax.all_gather(router, ("shard", "ctx"), axis=0, tiled=True),
        lax.all_gather(gain_one, ("shard", "ctx"), axis=0, tiled=True),
        lax.all_gather(gain_two, ("shard", "ctx"), axis=0, tiled=True),
    )
    scale_one = full_one.astype(jnp.float32)
    scale_two = full_two.astype(jnp.float32)
    inputs = tokens.astype(jnp.float32).reshape(count, width)
    normed_one, unit_one, inverse_one = norm_parts(inputs, scale_one)
    first_part = normed_one.astype(jnp.bfloat16)
    projected_rows = jnp.einsum(
        "td,kdf->tkf", first_part, full_qkv, preferred_element_type=jnp.float32
    ).astype(jnp.bfloat16)
    query = projected_rows[:, 0].reshape(slots, local_len, heads, HEAD_DIM)
    pairs = projected_rows[:, 1:].reshape(slots, local_len, 2 * head_width)
    start_state = (
        jnp.full((slots, local_len, heads), masked_score, jnp.float32),
        jnp.zeros((slots, local_len, heads), jnp.float32),
        jnp.zeros((slots, local_len, heads, HEAD_DIM), jnp.float32),
    )
    piece = lax.all_gather(pairs, "ctx", axis=1, tiled=True)
    piece_len = piece.shape[1]
    step_size = math.gcd(piece_len, key_block)

    def inner(number, state):
        top, total, accum = state
        offset = number * step_size
        block = lax.dynamic_slice_in_dim(piece, offset, step_size, 1)
        keys, values, allowed, scores = score_block(
            query, block, offset, query_places, lengths, heads
        )
        scores = jnp.where(allowed, scores, masked_score)
        new_top = jnp.maximum(top, jnp.max(scores, axis=-1))
        factor = jnp.exp(top - new_top)
        weights = jnp.where(allowed, jnp.exp(scores - new_top[..., None]), 0.0)
        total = total * factor + jnp.sum(weights, axis=-1)
        accum = accum * factor[..., None] + jnp.einsum(
            "sqhk,skhd->sqhd",
            weights.astype(jnp.bfloat16),
            values,
            preferred_element_type=jnp.float32,
        )
        return (new_top, total, accum)

    top, total, accum = lax.fori_loop(0, piece_len // step_size, inner, start_state)
    log_total = top + jnp.log(total)
    blended_layer_yield = (accum / total[..., None]).astype(jnp.bfloat16)
    mixed_rows = blended_layer_yield.reshape(count, head_width)
    partial_branch = jnp.einsum(
        "tf,df->td", mixed_rows, full_proj, preferred_element_type=jnp.float32
    )
    expert_path_yield = lax.psum(partial_branch.astype(jnp.bfloat16), "tp").astype(jnp.float32)
    middle = inputs + expert_path_yield
    normed_two, unit_two, inverse_two = norm_parts(middle, scale_two)
    second_part = normed_two.astype(jnp.bfloat16)
    router_logits = jnp.dot(second_part, full_router, preferred_element_type=jnp.float32)
    probs = jax.nn.softmax(router_logits, axis=-1)
    route = routes.reshape(count)
    valid = (query_places[None, :] < lengths[:, None]).reshape(count)
    expert_ids = jnp.arange(experts, dtype=jnp.int32)
    route_hot = route[:, None] == expert_ids[None, :]
    gate = jnp.sum(jnp.where(route_hot, probs, 0.0), axis=1)
    counted = (route_hot & valid[:, None]).astype(jnp.int32)
    earlier = jnp.cumsum(counted, axis=0) - counted
    place = jnp.sum(earlier * counted, axis=1)
    kept = valid & (place < capacity)
    target = jnp.where(kept, route * capacity + place, experts * capacity)
    send = (
        jnp.zeros((experts * capacity + 1, width), jnp.bfloat16)
        .at[target]
        .set(second_part)[:-1]
        .reshape(experts, capacity, width)
    )
    arrived_here = lax.all_to_all(send, ("shard", "ctx"), split_axis=0, concat_axis=0, tiled=True)
    sources, items, _ = arrived_here.shape
    arrived_rows = arrived_here.reshape(sources * items, width)
    pre = jnp.dot(arrived_rows, w_in[0], preferred_element_type=jnp.float32)
    hidden = jax.nn.gelu(pre).astype(jnp.bfloat16)
    partial_out = jnp.dot(hidden, w_out[0], preferred_element_type=jnp.float32)
    summed = lax.psum(partial_out.astype(jnp.bfloat16), "tp")
    going_back = lax.all_to_all(
        summed.reshape(sources, items, width),
        ("shard", "ctx"),
        split_axis=0,
        concat_axis=0,
        tiled=True,
    )
    pre_act = pre.reshape(sources, items, pre.shape[1])
    fetched = jnp.concatenate(
        [going_back.reshape(experts * capacity, width), jnp.zeros((1, width), jnp.bfloat16)], axis=0
    )[target]
    fetched_value = fetched.astype(jnp.float32)
    kept_value = kept.astype(jnp.float32)
    valid_value = valid.astype(jnp.float32)
    weighted_gate = kept_value * gate
    moe = weighted_gate[:, None] * fetched_value
    output = (
        (valid_value[:, None] * (middle + moe))
        .astype(jnp.bfloat16)
        .reshape(slots, local_len, width)
    )
    grad_out = valid_value[:, None] * cotangent.astype(jnp.float32).reshape(count, width)
    grad_fetched = (weighted_gate[:, None] * grad_out).astype(jnp.bfloat16)
    grad_send = (
        jnp.zeros((experts * capacity + 1, width), jnp.bfloat16)
        .at[target]
        .set(grad_fetched)[:-1]
        .reshape(experts, capacity, width)
    )
    grad_arrived = lax.all_to_all(
        grad_send, ("shard", "ctx"), split_axis=0, concat_axis=0, tiled=True
    )
    arrived_rows = arrived_here.reshape(-1, width)
    grad_rows = grad_arrived.reshape(-1, width)
    pre_rows = pre_act.reshape(arrived_rows.shape[0], pre_act.shape[2])
    hidden_rows = jax.nn.gelu(pre_rows).astype(jnp.bfloat16)
    grad_w_out = contract_rows(hidden_rows, grad_rows)[None]
    grad_hidden = contract_cols(grad_rows, w_out[0])
    unused_value, gelu_back = jax.vjp(jax.nn.gelu, pre_rows)
    grad_pre = gelu_back(grad_hidden)[0].astype(jnp.bfloat16)
    grad_w_in = contract_rows(arrived_rows, grad_pre)[None]
    partial_grad = contract_cols(grad_pre, w_in[0])
    grad_dispatched = lax.psum(partial_grad.astype(jnp.bfloat16), "tp")
    grad_home = lax.all_to_all(
        grad_dispatched.reshape(arrived_here.shape),
        ("shard", "ctx"),
        split_axis=0,
        concat_axis=0,
        tiled=True,
    )
    grad_home_rows = jnp.concatenate(
        [grad_home.reshape(experts * capacity, width), jnp.zeros((1, width), jnp.bfloat16)], axis=0
    )[target].astype(jnp.float32)
    grad_gate = kept_value * jnp.sum(grad_out * fetched_value, axis=1)
    grad_logits = ((grad_gate * gate)[:, None] * (route_hot.astype(jnp.float32) - probs)).astype(
        jnp.bfloat16
    )
    grad_router = contract_rows(second_part, grad_logits)
    grad_second = grad_home_rows + contract_cols(grad_logits, full_router)
    lifted_two, grad_gain_two = norm_back(grad_second, unit_two, inverse_two, scale_two)
    grad_middle = grad_out + lifted_two
    grad_branch = grad_middle.astype(jnp.bfloat16)
    grad_proj = contract_rows(grad_branch, mixed_rows)
    grad_mixed = (
        jnp.dot(grad_branch, full_proj, preferred_element_type=jnp.float32)
        .astype(jnp.bfloat16)
        .reshape(slots, local_len, heads, HEAD_DIM)
    )
    delta = jnp.sum(
        grad_mixed.astype(jnp.float32) * blended_layer_yield.astype(jnp.float32), axis=-1
    )
    every_pair = lax.all_gather(pairs, "ctx", axis=1, tiled=True)
    piece_len = every_pair.shape[1]
    key_step_size = math.gcd(piece_len, key_block)

    def inner(number, state):
        grad_query, grad_piece = state
        offset = number * key_step_size
        block = lax.dynamic_slice_in_dim(every_pair, offset, key_step_size, 1)
        keys, values, allowed, scores = score_block(
            query, block, 0 + offset, query_places, lengths, heads
        )
        weights = jnp.where(allowed, jnp.exp(scores - log_total[..., None]), 0.0)
        grad_values = jnp.einsum(
            "sqhk,sqhd->skhd",
            weights.astype(jnp.bfloat16),
            grad_mixed,
            preferred_element_type=jnp.float32,
        )
        grad_weights = jnp.einsum(
            "sqhd,skhd->sqhk", grad_mixed, values, preferred_element_type=jnp.float32
        )
        grad_scores = (weights * (grad_weights - delta[..., None])).astype(jnp.bfloat16)
        grad_query = (
            grad_query
            + jnp.einsum("sqhk,skhd->sqhd", grad_scores, keys, preferred_element_type=jnp.float32)
            * scale
        )
        grad_keys = (
            jnp.einsum("sqhk,sqhd->skhd", grad_scores, query, preferred_element_type=jnp.float32)
            * scale
        )
        update = jnp.concatenate(
            [
                grad_keys.reshape(slots, key_step_size, head_width),
                grad_values.reshape(slots, key_step_size, head_width),
            ],
            axis=-1,
        )
        return (grad_query, lax.dynamic_update_slice_in_dim(grad_piece, update, offset, 1))

    state = (
        jnp.zeros((slots, local_len, heads, HEAD_DIM), jnp.float32),
        jnp.zeros((slots, piece_len, 2 * head_width), jnp.float32),
    )
    grad_query_total, grad_all_pairs = lax.fori_loop(0, piece_len // key_step_size, inner, state)
    grad_pairs = lax.psum_scatter(
        grad_all_pairs.astype(jnp.bfloat16), "ctx", scatter_dimension=1, tiled=True
    )
    grad_query_rows = grad_query_total.astype(jnp.bfloat16).reshape(count, 1, head_width)
    grad_pair_rows = grad_pairs.reshape(count, 2, head_width)
    grad_projected = jnp.concatenate([grad_query_rows, grad_pair_rows], axis=1)
    grad_qkv = jnp.einsum(
        "td,tkf->kdf", first_part, grad_projected, preferred_element_type=jnp.float32
    )
    partial_first = jnp.einsum(
        "tkf,kdf->td", grad_projected, full_qkv, preferred_element_type=jnp.float32
    )
    grad_first = lax.psum(partial_first.astype(jnp.bfloat16), "tp").astype(jnp.float32)
    lifted_one, grad_gain_one = norm_back(grad_first, unit_one, inverse_one, scale_one)
    grad_tokens = (grad_middle + lifted_one).reshape(slots, local_len, width)
    shard_qkv, shard_proj, shard_router, shard_one, shard_two = (
        lax.psum_scatter(grad_qkv, ("shard", "ctx"), scatter_dimension=1, tiled=True),
        lax.psum_scatter(grad_proj, ("shard", "ctx"), scatter_dimension=0, tiled=True),
        lax.psum_scatter(grad_router, ("shard", "ctx"), scatter_dimension=0, tiled=True),
        lax.psum_scatter(grad_gain_one, ("shard", "ctx"), scatter_dimension=0, tiled=True),
        lax.psum_scatter(grad_gain_two, ("shard", "ctx"), scatter_dimension=0, tiled=True),
    )
    return (
        output,
        grad_tokens,
        shard_qkv,
        shard_proj,
        shard_router,
        shard_one,
        shard_two,
        grad_w_in,
        grad_w_out,
    )


def solution(mesh):
    return jax.shard_map(
        local,
        mesh=mesh,
        in_specs=(
            P("shard", "ctx", None),
            P("shard"),
            P("shard", "ctx", None),
            P(None, ("shard", "ctx"), "tp"),
            P(("shard", "ctx"), "tp"),
            P(("shard", "ctx"), None),
            P(("shard", "ctx")),
            P(("shard", "ctx")),
            P(("shard", "ctx"), None, "tp"),
            P(("shard", "ctx"), "tp", None),
            P("shard", "ctx", None),
        ),
        out_specs=(
            P("shard", "ctx", None),
            P("shard", "ctx", None),
            P(None, ("shard", "ctx"), "tp"),
            P(("shard", "ctx"), "tp"),
            P(("shard", "ctx"), None),
            P(("shard", "ctx")),
            P(("shard", "ctx")),
            P(("shard", "ctx"), None, "tp"),
            P(("shard", "ctx"), "tp", None),
        ),
        check_vma=False,
    )
```

profile of v0, /device:TPU:0, one launch (start us, length us, event | category | flops | bytes accessed | tf_op | source)
XLA Modules:
  0.0 1555.6 jit_solution(8912347346169904644)
XLA Ops:
  11.6 43.8 %all-reduce.8 = (bf16[1024]{0:T(1024)(128)(2,1)S(1)}, bf16[1024]{0:T(1024)(128)(2,1)S(1)}) all-reduce(bf16[1024]{0:T(1024)(128)(2,1)S(1)} %dynamic-update-slice.1, bf16[1024]{0:T(1024)(128)(2,1)S(1)} %dynamic-update-slice), channel_id=1, replica_groups=mesh['shard'=4,'ctx'=4,'tp'=2] {'shard','ctx'}, use_global_device_ids=true, to_apply=%add.3 | all-reduce | flops 2048 | bytes 8192
  59.8 21.7 %all-gather.5.cloned.1.call-done = bf16[3,1024,512]{2,1,0:T(8,128)(2,1)} async-done(((bf16[3,64,512]{2,1,0:T(8,128)(2,1)}), bf16[3,1024,512]{2,1,0:T(8,128)(2,1)}) %all-gather.5.cloned.1.call-update) | async-done | bytes 3145744 | tf_op jit(solution)/shard_map/all_gather | solution.py:80
  93.2 83.9 %all-gather.7.cloned.1.call-done = bf16[1,4096,1024]{1,2,0:T(8,128)(2,1)} async-done(((bf16[1,1024,1024]{1,2,0:T(8,128)(2,1)}), bf16[1,4096,1024]{1,2,0:T(8,128)(2,1)}) %all-gather.7.cloned.1.call-update) | async-done | bytes 8388624 | tf_op jit(solution)/shard_map/all_gather | solution.py:101
  177.1 133.8 %while.34 = (s32[]{:T(128)}, f32[1,1024,8]{1,2,0:T(8,128)S(1)}, f32[1,1024,8]{1,2,0:T(8,128)S(1)}, f32[1,1024,8,64]{1,3,2,0:T(8,128)}, s32[1]{0:T(128)}, /*index...) while((s32[]{:T(128)}, f32[1,1024,8]{1,2,0:T(8,128)S(1)}, ...), condition=%wide.region_5.6_spmd.clone, body=%wide.region_2.5_spmd.clone.sunk | while | flops 1130940928 | bytes 61355232 | solution.py:125
  323.7 15.8 %all-reduce.15.cloned.1.call-done = bf16[1024,1024]{1,0:T(8,128)(2,1)} async-done(((bf16[1024,1024]{1,0:T(8,128)(2,1)}), bf16[1024,1024]{1,0:T(8,128)(2,1)}) %all-reduce.15.cloned.1.call-update) | async-done | bytes 2097168 | tf_op jit(solution)/shard_map/psum | solution.py:132
  363.6 78.6 %all-gather = bf16[16,64,16]{1,2,0:T(8,128)(2,1)S(1)} all-gather(bf16[1,64,16]{1,2,0:T(8,128)(2,1)S(1)} %bitcast.394), channel_id=1, replica_groups=mesh['shard'=4,'ctx'=4,'tp'=2] {'shard','ctx'}, dimensions={0}, use_global_device_ids=true | all-gather | bytes 34816 | tf_op jit(solution)/shard_map/all_gather | solution.py:82
  456.3 10.4 all-to-all-start.2
  487.0 26.5 %all-to-all-done.2 = bf16[16,80,1024]{2,1,0:T(8,128)(2,1)} async-done(((bf16[16,80,1024]{2,1,0:T(8,128)(2,1)}), bf16[16,80,1024]{2,1,0:T(8,128)(2,1)}, u32[]{:S(2)}, u32[]{:S(2)}) %all-to-all-start.2) | async-done | bytes 2621472 | tf_op jit(solution)/shard_map/all_to_all | solution.py:190
  513.5 15.5 fusion.50
  536.3 35.1 %all-reduce.21.cloned.1.call-done = (bf16[16,80,1024]{2,1,0:T(8,128)(2,1)}, bf16[16,80,1024]{2,1,0:T(8,128)(2,1)}) async-done(((bf16[16,80,1024]{2,1,0:T(8,128)(2,1)}, bf16[16,80,1024]{2,1,0:T(8,128)(2,1)}), (bf16[16,80,1024]{2,1,0:T(8,128)(2,1)}, bf16[16,80,1024]{2,1,0:T(8,128)(2,1)})) %all-reduce.21.cloned.1.call-update) | async-done | bytes 5242896 | tf_op jit(solution)/shard_map/psum | solution.py:160
  571.4 67.3 %all_to_all.20 = bf16[16,80,1024]{2,1,0:T(8,128)(2,1)} all-to-all(bf16[16,80,1024]{2,1,0:T(8,128)(2,1)} %get-tuple-element.465), channel_id=1, replica_groups=mesh['shard'=4,'ctx'=4,'tp'=2] {'shard','ctx'}, dimensions={0} | all-to-all | bytes 5242880 | tf_op jit(solution)/shard_map/all_to_all | solution.py:204
  654.8 39.5 %all-to-all-done.1 = bf16[16,80,1024]{2,1,0:T(8,128)(2,1)} async-done(((bf16[16,80,1024]{2,1,0:T(8,128)(2,1)}), bf16[16,80,1024]{2,1,0:T(8,128)(2,1)}, u32[]{:S(2)}, u32[]{:S(2)}) %all-to-all-start.1) | async-done | bytes 2621472 | tf_op jit(solution)/shard_map/all_to_all | solution.py:161
  724.1 284.5 %while.35 = (s32[]{:T(128)}, f32[1,1024,8,64]{1,3,2,0:T(8,128)}, bf16[1,4096,1024]{1,2,0:T(8,128)(2,1)}, bf16[1,4096,1024]{1,2,0:T(8,128)(2,1)}, s32[1]{0:T(128)...) while((s32[]{:T(128)}, f32[1,1024,8,64]{1,3,2,0:T(8,128)}, ...), condition=%wide.region_24.25_spmd.clone, body=%wide.region_23.24_spmd.clone.sunk | while | flops 2731543040 | bytes 109163824 | solution.py:276
  779.8 9.5 fusion.179
  815.3 9.5 fusion.179
  850.8 9.5 fusion.179
  1015.4 86.0 %reduce-scatter.6.cloned.1.call-done = bf16[1,1024,1024]{1,2,0:T(8,128)(2,1)} async-done(((bf16[1,4096,1024]{1,2,0:T(8,128)(2,1)}), bf16[1,1024,1024]{1,2,0:T(8,128)(2,1)}) %reduce-scatter.6.cloned.1.call-update) | async-done | bytes 2097168 | tf_op jit(solution)/shard_map/reduce_scatter | solution.py:277
  1136.5 11.0 convolution_bitcast_fusion.1
  1147.5 12.3 convolution_bitcast_fusion
  1159.8 21.4 %reduce-scatter.10.cloned.1.call-done = f32[64,16]{1,0:T(8,128)} async-done(((f32[1024,16]{1,0:T(8,128)}), f32[64,16]{1,0:T(8,128)}) %reduce-scatter.10.cloned.1.call-update) | async-done | bytes 4112
  1182.6 18.6 %all-reduce.17.cloned.1.call-done = bf16[1024,1024]{1,0:T(8,128)(2,1)} async-done(((bf16[1024,1024]{1,0:T(8,128)(2,1)}), bf16[1024,1024]{1,0:T(8,128)(2,1)}) %all-reduce.17.cloned.1.call-update) | async-done | bytes 2097168 | tf_op jit(solution)/shard_map/psum | solution.py:289
  1204.7 44.8 %all-reduce.7 = (f32[1024]{0:T(1024)S(1)}, f32[1024]{0:T(1024)S(1)}) all-reduce(f32[1024]{0:T(1024)S(1)} %get-tuple-element.420, f32[1024]{0:T(1024)S(1)} %copy-done.33), channel_id=6, replica_groups=mesh['shard'=4,'ctx'=4,'tp'=2] {'shard','ctx'}, use_global_device_ids=true, to_apply=%region_33.34.clone | all-reduce | flops 2048 | bytes 16384
  1255.7 209.6 %all-reduce.19.cloned.1.call-done = f32[3,1024,512]{2,0,1:T(4,128)} async-done(((f32[3,1024,512]{2,0,1:T(4,128)}), f32[3,1024,512]{2,0,1:T(4,128)}) %all-reduce.19.cloned.1.call-update) | async-done | bytes 6291472
  1467.3 81.3 %reduce-scatter.8.cloned.1.call-done = f32[64,512]{1,0:T(8,128)} async-done(((f32[1024,512]{1,0:T(8,128)}), f32[64,512]{1,0:T(8,128)}) %reduce-scatter.8.cloned.1.call-update) | async-done | bytes 131088 | tf_op jit(solution)/shard_map/reduce_scatter | solution.py:294
  (385 shorter events, 585.3 us)
Async XLA Ops:
  7.2 74.3 %copy-start = (bf16[1,1024,1024]{2,1,0:T(8,128)(2,1)S(1)}, bf16[1,1024,1024]{2,1,0:T(8,128)(2,1)}, u32[]{:S(2)}) copy-start(bf16[1,1024,1024]{2,1,0:T(8,128)(2,1)} %param.15) | copy-start | bytes 6291460
  7.2 74.3 %all-gather.5.cloned.1.call-start = ((), (), s32[]{:S(2)}) async-start(), calls=%async_computation.7 | async-start | bytes 3342336 | tf_op jit(solution)/shard_map/all_gather | solution.py:80
  7.9 169.2 %all-gather.7.cloned.1.call-start = ((), (), s32[]{:S(2)}) async-start(), calls=%async_computation.8 | async-start | bytes 10485760 | tf_op jit(solution)/shard_map/all_gather | solution.py:101
  55.5 32.1 %copy-start.26 = (f32[1024]{0:T(1024)}, f32[1024]{0:T(1024)S(1)}, u32[]{:S(2)}) copy-start(f32[1024]{0:T(1024)S(1)} %convert_element_type.129) | copy-start | bytes 12292
  57.5 30.2 %copy-start.22 = (f32[1024]{0:T(1024)}, f32[1024]{0:T(1024)S(1)}, u32[]{:S(2)}) copy-start(f32[1024]{0:T(1024)S(1)} %broadcast_multiply_fusion.5) | copy-start | bytes 12292
  59.8 27.9 %copy-start.28 = (f32[1024]{0:T(1024)}, f32[1024]{0:T(1024)S(1)}, u32[]{:S(2)}) copy-start(f32[1024]{0:T(1024)S(1)} %add_rsqrt_fusion.1) | copy-start | bytes 12292
  90.8 222.9 %all-gather.9.cloned.1.call-start = ((), (), s32[]{:S(2)}) async-start(), calls=%async_computation.9 | async-start | bytes 1114112 | tf_op jit(solution)/shard_map/all_gather | solution.py:81
  91.6 247.8 %all-reduce.15.cloned.1.call-start = ((), (), s32[]{:S(2)}) async-start(), calls=%async_computation.10 | async-start | bytes 4194304 | tf_op jit(solution)/shard_map/psum | solution.py:132
  356.7 99.6 %all-to-all-start = ((bf16[16,80,1024]{2,1,0:T(8,128)(2,1)}), bf16[16,80,1024]{2,1,0:T(8,128)(2,1)}, u32[]{:S(2)}, u32[]{:S(2)}) async-start(bf16[16,80,1024]{2,1,0:T(8,128)(2,1)} %bitcast.365), calls=%async_computation | async-start | bytes 5242880 | tf_op jit(solution)/shard_map/all_to_all | solution.py:154
  444.6 264.5 %copy-start.16 = (f32[1024,16]{0,1:T(8,128)}, f32[1024,16]{0,1:T(8,128)S(1)}, u32[]{:S(2)}) copy-start(f32[1024,16]{0,1:T(8,128)S(1)} %get-tuple-element.481) | copy-start | bytes 196612
  444.6 264.5 %copy-start.20 = (f32[1024]{0:T(1024)}, f32[1024]{0:T(1024)S(1)}, u32[]{:S(2)}) copy-start(f32[1024]{0:T(1024)S(1)} %get-tuple-element.480) | copy-start | bytes 12292
  444.7 264.5 %copy-start.24 = (f32[1024]{0:T(1024)}, f32[1024]{0:T(1024)S(1)}, u32[]{:S(2)}) copy-start(f32[1024]{0:T(1024)S(1)} %fusion.112) | copy-start | bytes 12292
  456.3 57.2 %all-to-all-start.2 = ((bf16[16,80,1024]{2,1,0:T(8,128)(2,1)}), bf16[16,80,1024]{2,1,0:T(8,128)(2,1)}, u32[]{:S(2)}, u32[]{:S(2)}) async-start(bf16[16,80,1024]{2,1,0:T(8,128)(2,1)} %bitcast.367), calls=%async_computation.2 | async-start | bytes 5242880 | tf_op jit(solution)/shard_map/all_to_all | solution.py:190
  466.7 104.7 %all-reduce.21.cloned.1.call-start = ((), (), s32[]{:S(2)}) async-start(), calls=%async_computation.16 | async-start | bytes 10485760 | tf_op jit(solution)/shard_map/psum | solution.py:160
  466.7 12.6 copy-start.34
  513.5 15.5 copy-start.35
  638.7 55.6 %all-to-all-start.1 = ((bf16[16,80,1024]{2,1,0:T(8,128)(2,1)}), bf16[16,80,1024]{2,1,0:T(8,128)(2,1)}, u32[]{:S(2)}, u32[]{:S(2)}) async-start(bf16[16,80,1024]{2,1,0:T(8,128)(2,1)} %get-tuple-element.464), calls=%async_computation.1 | async-start | bytes 5242880 | tf_op jit(solution)/shard_map/all_to_all | solution.py:161
  643.2 458.2 %reduce-scatter.6.cloned.1.call-start = ((), (), s32[]{:S(2)}) async-start(), calls=%async_computation.11 | async-start | bytes 10485760 | tf_op jit(solution)/shard_map/reduce_scatter | solution.py:277
  1008.6 172.6 %reduce-scatter.10.cloned.1.call-start = ((), (), s32[]{:S(2)}) async-start(), calls=%async_computation.14 | async-start | bytes 557056
  1011.9 93.5 %copy-start.15 = (bf16[1024,1,512]{2,0,1:T(8,128)(2,1)S(1)}, bf16[1024,1,512]{2,0,1:T(8,128)(2,1)}, u32[]{:S(2)}) copy-start(bf16[1024,1,512]{2,0,1:T(8,128)(2,1)} %copy.50) | copy-start | bytes 3145732
  1015.3 185.9 %all-reduce.17.cloned.1.call-start = ((), (), s32[]{:S(2)}) async-start(), calls=%async_computation.12 | async-start | bytes 4194304 | tf_op jit(solution)/shard_map/psum | solution.py:289
  1112.8 352.4 %all-reduce.19.cloned.1.call-start = ((), (), s32[]{:S(2)}) async-start(), calls=%async_computation.15 | async-start | bytes 16777216
  1130.4 418.2 %reduce-scatter.8.cloned.1.call-start = ((), (), s32[]{:S(2)}) async-start(), calls=%async_computation.13 | async-start | bytes 2228224 | tf_op jit(solution)/shard_map/reduce_scatter | solution.py:294
  1159.8 44.9 %copy-start.33 = (f32[1024]{0:T(1024)S(1)}, f32[1024]{0:T(1024)}, u32[]{:S(2)}) copy-start(f32[1024]{0:T(1024)} %get-tuple-element.418) | copy-start | bytes 12292
  (42 other events, 142.1 us)
Sparse Core Ops, SparseCore 0:
  10.8 70.7 all-gather.4
  91.0 86.0 all-gather.6
  179.9 55.1 all-gather.8
  318.1 21.2 all-reduce.14
  536.4 34.9 all-reduce.20
  1008.7 92.6 reduce-scatter.5
  1103.7 77.4 reduce-scatter.9
  1183.6 17.6 all-reduce.16
  1207.3 257.9 all-reduce.18
  1468.0 80.5 reduce-scatter.7
where the time goes:
time: 1560 us
  waiting for transfers between devices  641 us (41%)
  matrix products  435 us (28%)
  blocking collectives  235 us (15%)
  local copies, waits for them, and re-layouts  103 us (7%)
  other arithmetic  100 us (6%)
  starting transfers between devices  22.4 us (1%)
  between operations  17.1 us (1%)
    unnamed x12, waiting for transfers between devices  232 us
    unnamed x2, blocking collectives  88.6 us
    dot_general x16, matrix products, score_block(): jnp.einsum('sqhd,skhd->sqhk', query, keys, preferred_element_type=jnp.flo...  87 us
    reduce_scatter x1, waiting for transfers between devices, local(): lax.psum_scatter(grad_all_pairs.astype(jnp.bfloat16), 'ctx', scatter_dime...  86 us
    all_gather x1, waiting for transfers between devices, local(): piece = lax.all_gather(pairs, 'ctx', axis=1, tiled=True)  83.9 us
    reduce_scatter x1, waiting for transfers between devices, local(): lax.psum_scatter(grad_proj, ('shard', 'ctx'), scatter_dimension=0, tiled=...  81.3 us
    all_gather x1, blocking collectives, local(): lax.all_gather(router, ('shard', 'ctx'), axis=0, tiled=True)  78.6 us
    dot_general x8, matrix products, inner(): jnp.einsum('sqhd,skhd->sqhk', grad_mixed, values, preferred_element_type=...  75.8 us
  transfers between devices with their start and end apart: 13, of which 11 were waited for; matrix products, arithmetic and copies ran while one was open for 17% of the time, Pallas kernels for 0%

commit v1 on v0

--- a/solution.py
+++ b/solution.py
@@ -158,13 +158,21 @@
     hidden = jax.nn.gelu(pre).astype(jnp.bfloat16)
     partial_out = jnp.dot(hidden, w_out[0], preferred_element_type=jnp.float32)
     summed = lax.psum(partial_out.astype(jnp.bfloat16), "tp")
-    going_back = lax.all_to_all(
-        summed.reshape(sources, items, width),
-        ("shard", "ctx"),
-        split_axis=0,
-        concat_axis=0,
-        tiled=True,
-    )
+    value = summed.reshape(sources, items, width)
+    ways, here = (lax.axis_size(("shard", "ctx")), lax.axis_index(("shard", "ctx")))
+    width_2 = value.shape[0] // ways
+    lengths_2 = list(value.shape)
+    lengths_2[0] = width_2
+    height = lengths_2[0]
+    lengths_2[0] = height * ways
+    going_back = jnp.zeros(lengths_2, value.dtype)
+    for mask in range(ways):
+        part = lax.dynamic_slice_in_dim(value, (here ^ mask) * width_2, width_2, axis=0)
+        if mask:
+            part = lax.ppermute(part, ("shard", "ctx"), [(d, d ^ mask) for d in range(ways)])
+        going_back = lax.dynamic_update_slice_in_dim(
+            going_back, part, (here ^ mask) * height, axis=0
+        )
     pre_act = pre.reshape(sources, items, pre.shape[1])
     fetched = jnp.concatenate(
         [going_back.reshape(experts * capacity, width), jnp.zeros((1, width), jnp.bfloat16)], axis=0

time: 1560 us -> 1570 us (level)
  blocking collectives: 235 us -> 167 us
  starting transfers between devices: 22.4 us -> 71.4 us
  waiting for transfers between devices: 641 us -> 667 us
    ppermute x0 -> x15, waiting for transfers between devices: none -> 73.6 us  [local(): lax.ppermute(part, ('shard', 'ctx'), [(d, d ^ mask) for d in range(ways)])]
    all_to_all x1 -> x0, blocking collectives: 67.3 us -> none  [local(): lax.all_to_all(grad_dispatched.reshape(arrived_here.shape), ('shard', 'ct...]
    ppermute x0 -> x15, starting transfers between devices: none -> 46.3 us  [local(): lax.ppermute(part, ('shard', 'ctx'), [(d, d ^ mask) for d in range(ways)])]
    all_to_all x1, waiting for transfers between devices: 39.5 us -> 0.01 us  [local(): lax.all_to_all(grad_dispatched.reshape(arrived_here.shape), ('shard', 'ct...]
  transfers between devices with their start and end apart: 13 -> 28, of which waited for: 11 -> 18; matrix products, arithmetic and copies ran while one was open for 17% -> 17% of each run, Pallas kernels for 0% -> 0%
where the time goes in v1:
time: 1570 us; the launch traced here: 1560 us
  waiting for transfers between devices  667 us (42%)
  matrix products  438 us (28%)
  blocking collectives  167 us (11%)
  local copies, waits for them, and re-layouts  102 us (6%)
  other arithmetic  100 us (6%)
  starting transfers between devices  71.4 us (5%)
  between operations  17.3 us (1%)
    unnamed x12, waiting for transfers between devices  233 us
    unnamed x2, blocking collectives  88.6 us
    dot_general x16, matrix products, score_block(): jnp.einsum('sqhd,skhd->sqhk', query, keys, preferred_element_type=jnp.flo...  87.2 us
    all_gather x1, waiting for transfers between devices, local(): piece = lax.all_gather(pairs, 'ctx', axis=1, tiled=True)  83.8 us
    reduce_scatter x1, waiting for transfers between devices, local(): lax.psum_scatter(grad_proj, ('shard', 'ctx'), scatter_dimension=0, tiled=...  81.3 us
    all_gather x1, blocking collectives, local(): lax.all_gather(router, ('shard', 'ctx'), axis=0, tiled=True)  78.6 us
    reduce_scatter x1, waiting for transfers between devices, local(): lax.psum_scatter(grad_all_pairs.astype(jnp.bfloat16), 'ctx', scatter_dime...  77.8 us
    dot_general x8, matrix products, inner(): jnp.einsum('sqhd,skhd->sqhk', grad_mixed, values, preferred_element_type=...  75.7 us
  transfers between devices with their start and end apart: 28, of which 18 were waited for; matrix products, arithmetic and copies ran while one was open for 17% of the time, Pallas kernels for 0%

profile of v1, /device:TPU:0, one launch (start us, length us, event | category | flops | bytes accessed | tf_op | source)
XLA Modules:
  0.0 1564.6 jit_solution(14631718573106760288)
XLA Ops:
  11.6 43.8 %all-reduce.8 = (bf16[1024]{0:T(1024)(128)(2,1)S(1)}, bf16[1024]{0:T(1024)(128)(2,1)S(1)}) all-reduce(bf16[1024]{0:T(1024)(128)(2,1)S(1)} %dynamic-update-slice.1, bf16[1024]{0:T(1024)(128)(2,1)S(1)} %dynamic-update-slice), channel_id=1, replica_groups=mesh['shard'=4,'ctx'=4,'tp'=2] {'shard','ctx'}, use_global_device_ids=true, to_apply=%add.3 | all-reduce | flops 2048 | bytes 8192
  59.8 21.7 %all-gather.5.cloned.1.call-done = bf16[3,1024,512]{2,1,0:T(8,128)(2,1)} async-done(((bf16[3,64,512]{2,1,0:T(8,128)(2,1)}), bf16[3,1024,512]{2,1,0:T(8,128)(2,1)}) %all-gather.5.cloned.1.call-update) | async-done | bytes 3145744 | tf_op jit(solution)/shard_map/all_gather | solution.py:80
  93.2 83.8 %all-gather.7.cloned.1.call-done = bf16[1,4096,1024]{1,2,0:T(8,128)(2,1)} async-done(((bf16[1,1024,1024]{1,2,0:T(8,128)(2,1)}), bf16[1,4096,1024]{1,2,0:T(8,128)(2,1)}) %all-gather.7.cloned.1.call-update) | async-done | bytes 8388624 | tf_op jit(solution)/shard_map/all_gather | solution.py:101
  177.1 133.9 %while.34 = (s32[]{:T(128)}, f32[1,1024,8]{1,2,0:T(8,128)S(1)}, f32[1,1024,8]{1,2,0:T(8,128)S(1)}, f32[1,1024,8,64]{1,3,2,0:T(8,128)}, s32[1]{0:T(128)}, /*index...) while((s32[]{:T(128)}, f32[1,1024,8]{1,2,0:T(8,128)S(1)}, ...), condition=%wide.region_5.6_spmd.clone, body=%wide.region_2.5_spmd.clone.sunk | while | flops 1130940928 | bytes 61355232 | solution.py:125
  323.8 15.8 %all-reduce.15.cloned.1.call-done = bf16[1024,1024]{1,0:T(8,128)(2,1)} async-done(((bf16[1024,1024]{1,0:T(8,128)(2,1)}), bf16[1024,1024]{1,0:T(8,128)(2,1)}) %all-reduce.15.cloned.1.call-update) | async-done | bytes 2097168 | tf_op jit(solution)/shard_map/psum | solution.py:132
  363.7 78.6 %all-gather = bf16[16,64,16]{1,2,0:T(8,128)(2,1)S(1)} all-gather(bf16[1,64,16]{1,2,0:T(8,128)(2,1)S(1)} %bitcast.394), channel_id=1, replica_groups=mesh['shard'=4,'ctx'=4,'tp'=2] {'shard','ctx'}, dimensions={0}, use_global_device_ids=true | all-gather | bytes 34816 | tf_op jit(solution)/shard_map/all_gather | solution.py:82
  456.4 10.4 all-to-all-start.1
  487.1 26.5 %all-to-all-done.1 = bf16[16,80,1024]{2,1,0:T(8,128)(2,1)} async-done(((bf16[16,80,1024]{2,1,0:T(8,128)(2,1)}), bf16[16,80,1024]{2,1,0:T(8,128)(2,1)}, u32[]{:S(2)}, u32[]{:S(2)}) %all-to-all-start.1) | async-done | bytes 2621472 | tf_op jit(solution)/shard_map/all_to_all | solution.py:198
  513.6 15.5 fusion.50
  536.4 35.1 %all-reduce.21.cloned.1.call-done = (bf16[16,80,1024]{2,1,0:T(8,128)(2,1)}, bf16[16,80,1024]{2,1,0:T(8,128)(2,1)}) async-done(((bf16[16,80,1024]{2,1,0:T(8,128)(2,1)}, bf16[16,80,1024]{2,1,0:T(8,128)(2,1)}), (bf16[16,80,1024]{2,1,0:T(8,128)(2,1)}, bf16[16,80,1024]{2,1,0:T(8,128)(2,1)})) %all-reduce.21.cloned.1.call-update) | async-done | bytes 5242896 | tf_op jit(solution)/shard_map/psum | solution.py:160
  594.0 14.5 collective-permute-done.1
  611.3 26.3 %collective-permute-done.3 = bf16[1,80,1024]{2,1,0:T(8,128)(2,1)S(1)} collective-permute-done((bf16[1,80,1024]{2,1,0:T(8,128)(2,1)S(1)}, bf16[1,80,1024]{2,1,0:T(8,128)(2,1)S(1)}, u32[]{:S(2)}, u32[]{:S(2)}) %collective-permute-start.3) | collective-permute-done | bytes 163872 | tf_op jit(solution)/shard_map/ppermute | solution.py:172
  660.0 14.5 collective-permute-done.7
  742.3 284.7 %while.35 = (s32[]{:T(128)}, f32[1,1024,8,64]{1,3,2,0:T(8,128)}, bf16[1,4096,1024]{1,2,0:T(8,128)(2,1)}, bf16[1,4096,1024]{1,2,0:T(8,128)(2,1)}, s32[1]{0:T(128)...) while((s32[]{:T(128)}, f32[1,1024,8,64]{1,3,2,0:T(8,128)}, ...), condition=%wide.region_24.25_spmd.clone, body=%wide.region_23.24_spmd.clone.sunk | while | flops 2731543040 | bytes 109163824 | solution.py:284
  762.5 9.5 fusion.179
  869.1 9.5 fusion.179
  1032.7 77.8 %reduce-scatter.6.cloned.1.call-done = bf16[1,1024,1024]{1,2,0:T(8,128)(2,1)} async-done(((bf16[1,4096,1024]{1,2,0:T(8,128)(2,1)}), bf16[1,1024,1024]{1,2,0:T(8,128)(2,1)}) %reduce-scatter.6.cloned.1.call-update) | async-done | bytes 2097168 | tf_op jit(solution)/shard_map/reduce_scatter | solution.py:285
  1145.6 10.8 convolution_bitcast_fusion.1
  1156.4 12.3 convolution_bitcast_fusion
  1168.7 21.6 %reduce-scatter.10.cloned.1.call-done = f32[64,16]{1,0:T(8,128)} async-done(((f32[1024,16]{1,0:T(8,128)}), f32[64,16]{1,0:T(8,128)}) %reduce-scatter.10.cloned.1.call-update) | async-done | bytes 4112
  1191.7 18.6 %all-reduce.17.cloned.1.call-done = bf16[1024,1024]{1,0:T(8,128)(2,1)} async-done(((bf16[1024,1024]{1,0:T(8,128)(2,1)}), bf16[1024,1024]{1,0:T(8,128)(2,1)}) %all-reduce.17.cloned.1.call-update) | async-done | bytes 2097168 | tf_op jit(solution)/shard_map/psum | solution.py:297
  1213.7 44.8 %all-reduce.7 = (f32[1024]{0:T(1024)S(1)}, f32[1024]{0:T(1024)S(1)}) all-reduce(f32[1024]{0:T(1024)S(1)} %get-tuple-element.420, f32[1024]{0:T(1024)S(1)} %copy-done.33), channel_id=6, replica_groups=mesh['shard'=4,'ctx'=4,'tp'=2] {'shard','ctx'}, use_global_device_ids=true, to_apply=%region_33.34.clone | all-reduce | flops 2048 | bytes 16384
  1264.7 209.6 %all-reduce.19.cloned.1.call-done = f32[3,1024,512]{2,0,1:T(4,128)} async-done(((f32[3,1024,512]{2,0,1:T(4,128)}), f32[3,1024,512]{2,0,1:T(4,128)}) %all-reduce.19.cloned.1.call-update) | async-done | bytes 6291472
  1476.3 81.3 %reduce-scatter.8.cloned.1.call-done = f32[64,512]{1,0:T(8,128)} async-done(((f32[1024,512]{1,0:T(8,128)}), f32[64,512]{1,0:T(8,128)}) %reduce-scatter.8.cloned.1.call-update) | async-done | bytes 131088 | tf_op jit(solution)/shard_map/reduce_scatter | solution.py:302
  (431 shorter events, 663.4 us)
Async XLA Ops:
  7.2 74.3 %all-gather.5.cloned.1.call-start = ((), (), s32[]{:S(2)}) async-start(), calls=%async_computation.6 | async-start | bytes 3342336 | tf_op jit(solution)/shard_map/all_gather | solution.py:80
  7.9 169.2 %all-gather.7.cloned.1.call-start = ((), (), s32[]{:S(2)}) async-start(), calls=%async_computation.7 | async-start | bytes 10485760 | tf_op jit(solution)/shard_map/all_gather | solution.py:101
  90.8 223.0 %all-gather.9.cloned.1.call-start = ((), (), s32[]{:S(2)}) async-start(), calls=%async_computation.8 | async-start | bytes 1114112 | tf_op jit(solution)/shard_map/all_gather | solution.py:81
  91.6 248.0 %all-reduce.15.cloned.1.call-start = ((), (), s32[]{:S(2)}) async-start(), calls=%async_computation.9 | async-start | bytes 4194304 | tf_op jit(solution)/shard_map/psum | solution.py:132
  356.8 99.6 %all-to-all-start = ((bf16[16,80,1024]{2,1,0:T(8,128)(2,1)}), bf16[16,80,1024]{2,1,0:T(8,128)(2,1)}, u32[]{:S(2)}, u32[]{:S(2)}) async-start(bf16[16,80,1024]{2,1,0:T(8,128)(2,1)} %bitcast.365), calls=%async_computation | async-start | bytes 5242880 | tf_op jit(solution)/shard_map/all_to_all | solution.py:154
  456.4 57.2 %all-to-all-start.1 = ((bf16[16,80,1024]{2,1,0:T(8,128)(2,1)}), bf16[16,80,1024]{2,1,0:T(8,128)(2,1)}, u32[]{:S(2)}, u32[]{:S(2)}) async-start(bf16[16,80,1024]{2,1,0:T(8,128)(2,1)} %bitcast.367), calls=%async_computation.1 | async-start | bytes 5242880 | tf_op jit(solution)/shard_map/all_to_all | solution.py:198
  466.8 104.7 %all-reduce.21.cloned.1.call-start = ((), (), s32[]{:S(2)}) async-start(), calls=%async_computation.15 | async-start | bytes 10485760 | tf_op jit(solution)/shard_map/psum | solution.py:160
  571.5 142.3 %all-to-all-start.2 = ((bf16[16,80,1024]{2,1,0:T(8,128)(2,1)}), bf16[16,80,1024]{2,1,0:T(8,128)(2,1)}, u32[]{:S(2)}, u32[]{:S(2)}) async-start(bf16[16,80,1024]{2,1,0:T(8,128)(2,1)} %get-tuple-element.465), calls=%async_computation.2 | async-start | bytes 5242880 | tf_op jit(solution)/shard_map/all_to_all | solution.py:212
  578.4 532.1 %reduce-scatter.6.cloned.1.call-start = ((), (), s32[]{:S(2)}) async-start(), calls=%async_computation.10 | async-start | bytes 10485760 | tf_op jit(solution)/shard_map/reduce_scatter | solution.py:285
  580.7 27.8 %collective-permute-start.1 = (bf16[1,80,1024]{2,1,0:T(8,128)(2,1)S(1)}, bf16[1,80,1024]{2,1,0:T(8,128)(2,1)S(1)}, u32[]{:S(2)}, u32[]{:S(2)}) collective-permute-start(bf16[1,80,1024]{2,1,0:T(8,128)(2,1)S(1)} %get-tuple-element.491), channel_id=1, source_target_pairs={{0,4},{2,6},{4,0},{6,2},{8,12},{10,14},{12,8},{14,10},{16,20},{18,... | collective-permute-start | bytes 491528 | tf_op jit(solution)/shard_map/ppermute | solution.py:172
  584.1 116.8 %collective-permute-start.14 = (bf16[1,80,1024]{2,1,0:T(8,128)(2,1)S(1)}, bf16[1,80,1024]{2,1,0:T(8,128)(2,1)S(1)}, u32[]{:S(2)}, u32[]{:S(2)}) collective-permute-start(bf16[1,80,1024]{2,1,0:T(8,128)(2,1)S(1)} %get-tuple-element.478), channel_id=1, source_target_pairs={{0,30},{2,28},{4,26},{6,24},{8,22},{10,20},{12,18},{14,16},{16,14}... | collective-permute-start | bytes 491528 | tf_op jit(solution)/shard_map/ppermute | solution.py:172
  587.4 113.4 %collective-permute-start.13 = (bf16[1,80,1024]{2,1,0:T(8,128)(2,1)S(1)}, bf16[1,80,1024]{2,1,0:T(8,128)(2,1)S(1)}, u32[]{:S(2)}, u32[]{:S(2)}) collective-permute-start(bf16[1,80,1024]{2,1,0:T(8,128)(2,1)S(1)} %get-tuple-element.479), channel_id=1, source_target_pairs={{0,28},{2,30},{4,24},{6,26},{8,20},{10,22},{12,16},{14,18},{16,12}... | collective-permute-start | bytes 491528 | tf_op jit(solution)/shard_map/ppermute | solution.py:172
  588.9 111.9 %collective-permute-start.12 = (bf16[1,80,1024]{2,1,0:T(8,128)(2,1)S(1)}, bf16[1,80,1024]{2,1,0:T(8,128)(2,1)S(1)}, u32[]{:S(2)}, u32[]{:S(2)}) collective-permute-start(bf16[1,80,1024]{2,1,0:T(8,128)(2,1)S(1)} %get-tuple-element.480), channel_id=1, source_target_pairs={{0,26},{2,24},{4,30},{6,28},{8,18},{10,16},{12,22},{14,20},{16,10}... | collective-permute-start | bytes 491528 | tf_op jit(solution)/shard_map/ppermute | solution.py:172
  593.0 15.5 collective-permute-start.2
  608.5 29.1 %collective-permute-start.3 = (bf16[1,80,1024]{2,1,0:T(8,128)(2,1)S(1)}, bf16[1,80,1024]{2,1,0:T(8,128)(2,1)S(1)}, u32[]{:S(2)}, u32[]{:S(2)}) collective-permute-start(bf16[1,80,1024]{2,1,0:T(8,128)(2,1)S(1)} %get-tuple-element.489), channel_id=1, source_target_pairs={{0,8},{2,10},{4,12},{6,14},{8,0},{10,2},{12,4},{14,6},{16,24},{18,... | collective-permute-start | bytes 491528 | tf_op jit(solution)/shard_map/ppermute | solution.py:172
  608.5 33.6 %collective-permute-start.4 = (bf16[1,80,1024]{2,1,0:T(8,128)(2,1)S(1)}, bf16[1,80,1024]{2,1,0:T(8,128)(2,1)S(1)}, u32[]{:S(2)}, u32[]{:S(2)}) collective-permute-start(bf16[1,80,1024]{2,1,0:T(8,128)(2,1)S(1)} %get-tuple-element.488), channel_id=1, source_target_pairs={{0,10},{2,8},{4,14},{6,12},{8,2},{10,0},{12,6},{14,4},{16,26},{18,... | collective-permute-start | bytes 491528 | tf_op jit(solution)/shard_map/ppermute | solution.py:172
  648.8 25.7 %collective-permute-start.7 = (bf16[1,80,1024]{2,1,0:T(8,128)(2,1)S(1)}, bf16[1,80,1024]{2,1,0:T(8,128)(2,1)S(1)}, u32[]{:S(2)}, u32[]{:S(2)}) collective-permute-start(bf16[1,80,1024]{2,1,0:T(8,128)(2,1)S(1)} %get-tuple-element.485), channel_id=1, source_target_pairs={{0,16},{2,18},{4,20},{6,22},{8,24},{10,26},{12,28},{14,30},{16,0},... | collective-permute-start | bytes 491528 | tf_op jit(solution)/shard_map/ppermute | solution.py:172
  654.5 31.1 %collective-permute-start.8 = (bf16[1,80,1024]{2,1,0:T(8,128)(2,1)S(1)}, bf16[1,80,1024]{2,1,0:T(8,128)(2,1)S(1)}, u32[]{:S(2)}, u32[]{:S(2)}) collective-permute-start(bf16[1,80,1024]{2,1,0:T(8,128)(2,1)S(1)} %get-tuple-element.484), channel_id=1, source_target_pairs={{0,18},{2,16},{4,22},{6,20},{8,26},{10,24},{12,30},{14,28},{16,2},... | collective-permute-start | bytes 491528 | tf_op jit(solution)/shard_map/ppermute | solution.py:172
  674.5 19.1 %collective-permute-start.9 = (bf16[1,80,1024]{2,1,0:T(8,128)(2,1)S(1)}, bf16[1,80,1024]{2,1,0:T(8,128)(2,1)S(1)}, u32[]{:S(2)}, u32[]{:S(2)}) collective-permute-start(bf16[1,80,1024]{2,1,0:T(8,128)(2,1)S(1)} %get-tuple-element.483), channel_id=1, source_target_pairs={{0,20},{2,22},{4,16},{6,18},{8,28},{10,30},{12,24},{14,26},{16,4},... | collective-permute-start | bytes 491528 | tf_op jit(solution)/shard_map/ppermute | solution.py:172
  685.5 13.3 collective-permute-start.10
  1027.0 163.2 %reduce-scatter.10.cloned.1.call-start = ((), (), s32[]{:S(2)}) async-start(), calls=%async_computation.13 | async-start | bytes 557056
  1031.2 179.1 %all-reduce.17.cloned.1.call-start = ((), (), s32[]{:S(2)}) async-start(), calls=%async_computation.11 | async-start | bytes 4194304 | tf_op jit(solution)/shard_map/psum | solution.py:297
  1121.9 352.4 %all-reduce.19.cloned.1.call-start = ((), (), s32[]{:S(2)}) async-start(), calls=%async_computation.14 | async-start | bytes 16777216
  1139.5 418.1 %reduce-scatter.8.cloned.1.call-start = ((), (), s32[]{:S(2)}) async-start(), calls=%async_computation.12 | async-start | bytes 2228224 | tf_op jit(solution)/shard_map/reduce_scatter | solution.py:302
  (57 other events, 1348.2 us)
Sparse Core Ops, SparseCore 0:
  10.8 70.7 all-gather.4
  91.0 86.0 all-gather.6
  179.9 55.1 all-gather.8
  318.2 21.2 all-reduce.14
  536.5 34.9 all-reduce.20
  1027.1 83.2 reduce-scatter.5
  1112.7 77.4 reduce-scatter.9
  1192.6 17.6 all-reduce.16
  1216.3 257.9 all-reduce.18
  1477.0 80.5 reduce-scatter.7
